TPU v7x, 32 devices: a whole 2x2x4 slice. The times are simulated.
32 devices in a mesh: elem: 8 (over y, x, core), mode: 4 (over z).
Axes of the slice: x: 2, y: 2, z: 4, core: 2. Of those that a mesh axis runs over, the one named last changes fastest.
Arguments:
- velocity: float32 [3, 5184, 2, 512], P(None, 'elem', None, 'mode'), may hold values from -3 to 3
- column_width: float32 [8], P('elem'), may hold values from 0.5 to 2
- row_height: float32 [8], replicated, may hold values from 0.5 to 2
- disc_mask: int32 [64], P('elem'), may hold values from 0 to 1, as said below
Outputs:
- velocity_new: float32 [3, 5184, 2, 512], P(None, 'elem', None, 'mode')
Inputs may be any that keep to these rules, and one draw needn't show every extreme that they name: `disc_mask`: in each column of 8 elements the ones form one run of 2 to 4 consecutive rows, counted cyclically in y.
All inputs are finite; a program needn't handle non-finite values.
Results may differ from a plain program's by a relative error of at most 0.0001.
Values sent between devices are 32-bit elements; how exact they have to be, the bound alone decides.
A program may use at most 128 MiB of HBM per device.

v0:
```python
import math
import jax
import jax.numpy as jnp
import numpy as np
from jax import lax
from jax.sharding import PartitionSpec as P

ORDER = 8
ITERS = 2
gll_points = [
    -1.0,
    -0.8997579954114602,
    -0.6771862795107377,
    -0.3631174638261782,
    0.0,
    0.3631174638261782,
    0.6771862795107377,
    0.8997579954114602,
    1.0,
]
gll_weights = [
    0.0277777777777778,
    0.1654953615608055,
    0.2745387125001617,
    0.3464285109730463,
    0.3715192743764172,
    0.3464285109730463,
    0.2745387125001617,
    0.1654953615608055,
    0.0277777777777778,
]
viscosity = 0.5
time_step = 0.02
thrust_coef = 4.0 / 3.0
highest = lax.Precision.HIGHEST


def padded(shard, sides, width):
    for axis, dim in sides:
        peers, length = (lax.axis_size(axis), shard.shape[dim])
        up = [(i, (i + 1) % peers) for i in range(peers)]
        down = [(j, i) for i, j in up]
        last = lax.slice_in_dim(shard, length - width, length, axis=dim)
        initial = lax.slice_in_dim(shard, 0, width, axis=dim)
        before = lax.ppermute(last, axis, up)
        after = lax.ppermute(initial, axis, down)
        shard = jnp.concatenate([before, shard, after], axis=dim)
    return shard


def node_tables():
    points = np.array(gll_points)
    identity = np.eye(9)
    differences = points[:, None] - points[None, :] + identity
    barycentric = 1.0 / np.prod(differences, axis=1)
    off_diagonal = barycentric[None, :] / barycentric[:, None] / differences * (1.0 - identity)
    derivative = off_diagonal - identity * off_diagonal.sum(axis=1)[:, None]
    return (
        jnp.asarray(derivative, dtype=jnp.float32),
        jnp.asarray(np.array(gll_weights), dtype=jnp.float32),
    )


def spectral_tables(mode_count):
    planes = 3 * mode_count
    wave_index = jnp.arange(mode_count, dtype=jnp.int32)
    plane_index = jnp.arange(planes, dtype=jnp.int32)
    phase_index = wave_index[:, None] * plane_index[None, :] % planes
    angles = 2.0 * math.pi / planes * phase_index.astype(jnp.float32)
    cosine_table = jnp.cos(angles)
    sine_table = jnp.sin(angles)
    mode_weight = jnp.where(wave_index == 0, 1.0, 2.0).astype(jnp.float32)[:, None] / math.sqrt(
        mode_count
    )
    wave_number = 8.0 / mode_count * wave_index.astype(jnp.float32)[:, None]
    inverse = jnp.concatenate([mode_weight * cosine_table, -mode_weight * sine_table], axis=0)
    spanwise = jnp.concatenate(
        [-wave_number * mode_weight * sine_table, -wave_number * mode_weight * cosine_table], axis=0
    )
    forward = (
        math.sqrt(mode_count) / planes * jnp.concatenate([cosine_table, -sine_table], axis=0).T
    )
    return (inverse, spanwise, forward)


def assemble(nodal_field):
    extended = padded(nodal_field, (("elem", 2),), 1)
    first_layer = nodal_field[:, :, 0] + extended[:, :, 0]
    last_layer = nodal_field[:, :, 8] + extended[:, :, 10]
    nodal_field = jnp.concatenate(
        [first_layer[:, :, None], nodal_field[:, :, 1:8], last_layer[:, :, None]], axis=2
    )
    upper_layer = nodal_field[:, :, :, 8] + jnp.roll(nodal_field[:, :, :, 0], -1, axis=1)
    return jnp.concatenate(
        [
            jnp.roll(upper_layer, 1, axis=1)[:, :, :, None],
            nodal_field[:, :, :, 1:8],
            upper_layer[:, :, :, None],
        ],
        axis=3,
    )


def apply_operator(nodal_field, derivative, quad_weights, ratio_x, ratio_y, jacobian, factor):
    grad_r = jnp.einsum("ij,pejbl->peibl", derivative, nodal_field, precision=highest)
    grad_s = jnp.einsum("ij,peajl->peail", derivative, nodal_field, precision=highest)
    flux_r = grad_r * quad_weights[None, None, :, :, None] * ratio_x[None, :, None, None, None]
    flux_s = grad_s * quad_weights[None, None, :, :, None] * ratio_y[None, :, None, None, None]
    stiffness = jnp.einsum("ji,pejbl->peibl", derivative, flux_r, precision=highest) + jnp.einsum(
        "ji,peajl->peail", derivative, flux_s, precision=highest
    )
    masses = (
        jacobian[None, :, None, None, None] * quad_weights[None, None, :, :, None] * nodal_field
    )
    return assemble(factor * masses + viscosity * stiffness)


def weighted_sum(left_field, right_field, multiplicity):
    return jnp.sum(left_field * right_field * multiplicity[None, None, :, :, None], axis=(1, 2, 3))


def paired(residual, image_field, multiplicity):
    return lax.psum(
        (
            weighted_sum(residual, residual, multiplicity),
            weighted_sum(residual, image_field, multiplicity),
        ),
        "elem",
    )


def on_device(velocity, column_width, row_height, disc_mask):
    derivative, weights = node_tables()
    quad_weights = weights[:, None] * weights[None, :]
    node_index = jnp.arange(9)
    edge_count = jnp.where((node_index == 0) | (node_index == 8), 2.0, 1.0).astype(jnp.float32)
    multiplicity = 1.0 / (edge_count[:, None] * edge_count[None, :])
    groups = lax.axis_size("mode")
    local_modes = velocity.shape[3]
    mode_count = groups * local_modes
    planes = 3 * mode_count
    elements = velocity.shape[1] // 81
    local_elems = elements // groups
    col_width = column_width[0]
    inverse, spanwise, forward = spectral_tables(mode_count)
    nodal_field = velocity.reshape(3, elements, 9, 9, 2 * local_modes)
    mode_index = lax.axis_index("mode") * local_modes + jnp.arange(local_modes, dtype=jnp.int32)
    wavenumber = 8.0 / mode_count * mode_index.astype(jnp.float32)
    elem_start = lax.axis_index("mode") * local_elems
    local_heights = lax.dynamic_slice_in_dim(row_height, elem_start, local_elems)
    local_disc = lax.dynamic_slice_in_dim(disc_mask, elem_start, local_elems).astype(jnp.float32)
    members = lax.all_to_all(velocity, "mode", split_axis=1, concat_axis=3, tiled=True)
    flat_items = members.reshape(members.shape[0], members.shape[1], 2 * mode_count)
    values = jnp.einsum("pnl,lq->pnq", flat_items, inverse, precision=highest)
    along_z = jnp.einsum("pnl,lq->pnq", flat_items, spanwise, precision=highest)
    values = values.reshape(3, local_elems, 9, 9, planes)
    along_z = along_z.reshape(3, local_elems, 9, 9, planes)
    along_x = 2.0 / col_width * jnp.einsum("ij,pejbq->peibq", derivative, values, precision=highest)
    along_y = (2.0 / local_heights)[None, :, None, None, None] * jnp.einsum(
        "ij,peajq->peaiq", derivative, values, precision=highest
    )
    advection = values[0][None] * along_x + values[1][None] * along_y + values[2][None] * along_z
    plane_index = jnp.arange(planes)
    in_disc = ((plane_index >= 3 * planes // 8) & (plane_index < 5 * planes // 8)).astype(
        jnp.float32
    )
    disc_planes = 5 * planes // 8 - 3 * planes // 8
    local_jacobian = col_width * local_heights / 4.0
    node_weight = (local_disc * local_jacobian)[:, None, None] * quad_weights[None]
    partial_total = jnp.sum(node_weight[:, :, :, None] * values[0] * values[0] * in_disc)
    disc_total = lax.psum(partial_total, "mode")
    disc_area = disc_planes * col_width * jnp.sum(disc_mask.astype(jnp.float32) * row_height)
    pressure = disc_total / disc_area
    thrust = (
        -(0.5 * thrust_coef * ORDER)
        * pressure
        / col_width
        * local_disc[:, None, None, None]
        * in_disc
    )
    tendency = jnp.concatenate([(thrust - advection[0])[None], -advection[1:]], axis=0)
    spectral = jnp.einsum("peabq,ql->peabl", tendency, forward, precision=highest)
    spectral = spectral.reshape(3, local_elems * 81, 2, mode_count)
    returned = lax.all_to_all(spectral, "mode", split_axis=3, concat_axis=1, tiled=True)
    u_star = nodal_field + time_step * returned.reshape(3, elements, 9, 9, 2 * local_modes)
    jacobian = col_width * row_height / 4.0
    ratio_x = row_height / col_width
    ratio_y = col_width / row_height
    single = 1.0 / time_step + viscosity * wavenumber * wavenumber
    factor = jnp.concatenate([single, single])
    right_side = (
        assemble(
            jacobian[None, :, None, None, None] * quad_weights[None, None, :, :, None] * u_star
        )
        / time_step
    )
    residual = right_side
    solution = jnp.zeros_like(right_side)
    image_field = apply_operator(
        residual, derivative, quad_weights, ratio_x, ratio_y, jacobian, factor
    )
    norm_now, product = paired(residual, image_field, multiplicity)
    step_size = norm_now / product
    direction = residual
    along_image = image_field
    for iteration in range(ITERS):
        solution = solution + step_size[:, None, None, None, :] * direction
        residual = residual - step_size[:, None, None, None, :] * along_image
        if iteration + 1 < ITERS:
            image_field = apply_operator(
                residual, derivative, quad_weights, ratio_x, ratio_y, jacobian, factor
            )
            norm_next, product = paired(residual, image_field, multiplicity)
            beta_ratio = norm_next / norm_now
            step_size = norm_next / (product - beta_ratio * norm_next / step_size)
            direction = residual + beta_ratio[:, None, None, None, :] * direction
            along_image = image_field + beta_ratio[:, None, None, None, :] * along_image
            norm_now = norm_next
    return solution.reshape(3, elements * 81, 2, local_modes)


def solution(mesh):
    return jax.shard_map(
        on_device,
        mesh=mesh,
        in_specs=(P(None, "elem", None, "mode"), P("elem"), P(), P("elem")),
        out_specs=P(None, "elem", None, "mode"),
        check_vma=False,
    )
```

profile of v0, /device:TPU:0, one launch (start us, length us, event | category | flops | bytes accessed | tf_op | source)
XLA Modules:
  0.0 403.9 jit_solution(6718678095885858187)
XLA Ops:
  3.6 6.3 %all-to-all-start = ((f32[3,648,2,128]{3,2,0,1:T(2,128)}), f32[3,648,2,128]{3,2,0,1:T(2,128)S(1)}, u32[]{:S(2)}, u32[]{:S(2)}) async-start(f32[3,648,2,128]{3,2,0,1:T(2,128)} %copy.119), calls=%async_computation | async-start | bytes 3981312 | tf_op jit(solution)/shard_map/all_to_all | solution.py:152
  13.6 14.0 %fusion.61 = (f32[512,1536]{1,0:T(8,128)}, f32[512,1536]{1,0:T(8,128)}) fusion(), kind=kLoop, calls=%fused_computation.87 | loop fusion | flops 7864320 | bytes 6291456 | tf_op jit(solution)/shard_map/cos | solution.py:70
  27.5 14.2 %fusion.63 = (f32[512,1536]{1,0:T(8,128)}, f32[512,1536]{1,0:T(8,128)}) fusion(f32[512]{0:T(512)S(1)} %negate_multiply_fusion), kind=kLoop, calls=%fused_computation.89 | loop fusion | flops 8650752 | bytes 6293504 | tf_op jit(solution)/shard_map/mul | solution.py:78
  41.7 14.2 %fusion.64 = (f32[512,1536]{1,0:T(8,128)}, f32[512,1536]{1,0:T(8,128)}) fusion(f32[512]{0:T(512)S(1)} %fusion.77, f32[512]{0:T(512)S(1)} %select_multiply_fusion), kind=kLoop, calls=%fused_computation.90 | loop fusion | flops 8650752 | bytes 6295552 | tf_op jit(solution)/shard_map/mul | solution.py:76
  61.3 13.4 %fusion.54 = f32[3,162,1536]{2,1,0:T(8,128)S(1)} fusion(f32[3,162,1024]{2,1,0:T(8,128)} %reshape.205, f32[512,1536]{1,0:T(8,128)S(1)} %copy-done.11, f32[512,1536]{1,0:T(8,128)} %get-tuple-element.64), kind=kOutput, calls=%fused_computation.79 | convolution fusion | flops 9174515712 | bytes 11268096 | tf_op jit(solution)/shard_map/pnl,lq->pnq/dot_general | solution.py:154
  92.9 13.4 %fusion.53 = f32[3,162,1536]{2,1,0:T(8,128)S(1)} fusion(f32[3,162,1024]{2,1,0:T(8,128)} %reshape.205, f32[512,1536]{1,0:T(8,128)} %get-tuple-element.56, f32[512,1536]{1,0:T(8,128)S(1)} %copy-done.10), kind=kOutput, calls=%fused_computation.78 | convolution fusion | flops 9174515712 | bytes 11268096 | tf_op jit(solution)/shard_map/pnl,lq->pnq/dot_general | solution.py:155
  110.6 12.8 %psum.35 = f32[]{:T(128)} all-reduce(f32[]{:T(128)} %get-tuple-element.35), channel_id=1, replica_groups=mesh['elem'=8,'mode'=4] {'mode'}, use_global_device_ids=true, to_apply=%region_1.2 | all-reduce | flops 1 | bytes 8 | tf_op jit(solution)/shard_map/psum | solution.py:171
  125.6 11.5 %fusion.16 = f32[3,2,9,1536,9]{3,4,2,1,0:T(8,128)} fusion(f32[9,9,1,1,1]{1,0,4,3,2:T(8,128)S(1)} %copy-done.13, f32[3,2,9,9,1536]{4,0,3,2,1:T(4,128)} %bitcast.137), kind=kOutput, calls=%fused_computation.24 | convolution fusion | flops 80621568 | bytes 5972292 | tf_op jit(solution)/shard_map/ij,peajq->peaiq/dot_general | solution.py:159
  137.1 14.2 %fusion.15 = f32[3,2,9,9,1536]{4,2,3,1,0:T(8,128)S(1)} fusion(f32[3,2,9,9,1536]{4,0,3,2,1:T(4,128)S(1)} %bitcast.139, f32[3,2,9,1536,9]{3,4,2,1,0:T(8,128)} %fusion.16, f32[9,9,1,1,1]{1,0,4,3,2:T(8,128)S(1)} %copy-done.13, f32[3,2,9,9,1536]{4,0,3,2,1:T(4,128)S(1)} %bitcast.138, f32[2,9,9,1536]{3,1,2,0:T(8,128)S(1)} %copy-done.3, f32[2]{0:T(128)S(1)} %copy-done.30, ...), kind=kOutput, calls=%fused_computation.20 | convolution fusion | flops 85847040 | bytes 14930256 | tf_op jit(solution)/shard_map/ij,pejbq->peibq/dot_general | solution.py:158
  154.3 17.1 %fusion.7 = f32[3,2,9,9,1024]{4,2,3,1,0:T(8,128)S(1)} fusion(f32[512,1536]{1,0:T(8,128)S(1)} %copy-done.9, f32[512,1536]{1,0:T(8,128)S(1)} %copy-done.8, f32[2,2,9,9,1536]{4,2,3,1,0:T(8,128)S(1)} %slice_negate_fusion, f32[1,2,9,9,1536]{4,2,3,1,0:T(8,128)S(1)} %slice_subtract_fusion), kind=kOutput, calls=%fused_computation.10 | convolution fusion | flops 9176835072 | bytes 11268096 | tf_op jit(solution)/shard_map/peabq,ql->peabl/dot_general | solution.py:182
  176.0 6.6 %copy.132 = f32[3,162,2,512]{1,2,0,3:T(2,128)} copy(f32[3,162,2,512]{3,2,0,1:T(2,128)} %reshape.208) | data formatting | bytes 3981312 | tf_op jit(solution)/shard_map/reshape | solution.py:183
  192.3 63.4 %all-to-all-done.1 = f32[3,162,2,512]{1,2,0,3:T(2,128)} async-done(((f32[3,162,2,512]{1,2,0,3:T(2,128)}), f32[3,162,2,512]{1,2,0,3:T(2,128)}, u32[]{:S(2)}, u32[]{:S(2)}) %all-to-all-start.1) | async-done | bytes 1990688 | tf_op jit(solution)/shard_map/all_to_all | solution.py:184
  255.6 5.2 %broadcast_multiply_fusion = f32[3,162,2,512]{1,2,0,3:T(2,128)} fusion(f32[3,162,2,512]{1,2,0,3:T(2,128)} %all-to-all-done.1), kind=kLoop, calls=%fused_computation.101 | loop fusion | flops 497664 | bytes 3981312 | tf_op jit(solution)/shard_map/mul | solution.py:185
  260.8 6.4 %copy.133 = f32[3,162,2,4,128]{4,2,0,1,3:T(2,128)} copy(f32[3,162,2,4,128]{1,2,0,4,3:T(2,128)} %bitcast.140) | data formatting | bytes 3981312 | tf_op jit(solution)/shard_map/mul | solution.py:185
  267.2 4.7 %mul.655 = f32[3,8,9,9,256]{4,0,3,2,1:T(4,128)} reshape(f32[3,4,162,2,128]{4,3,0,2,1:T(2,128)} %bitcast.143) | data formatting | bytes 3981312 | tf_op jit(solution)/shard_map/mul | solution.py:185
  285.0 4.9 %fusion.44 = f32[3,8,9,256,9]{3,4,2,1,0:T(8,128)S(1)} fusion(f32[9,9,1,1,1]{1,0,4,3,2:T(8,128)S(1)} %copy-done.13, f32[3,8,9,9,256]{4,2,3,1,0:T(8,128)S(1)} %copy_multiply_fusion.4), kind=kOutput, calls=%fused_computation.64 | convolution fusion | flops 53747712 | bytes 3981636 | tf_op jit(solution)/shard_map/ij,peajl->peail/dot_general | solution.py:106
  298.2 5.9 %fusion.32 = f32[3,8,9,9,256]{4,2,0,1,3:T(8,128)S(1)} fusion(f32[3,8,9,256,9]{3,4,2,1,0:T(8,128)S(1)} %fusion.33, f32[8,9,9]{1,0,2:T(8,128)S(1)} %copy-done.22, f32[256]{0:T(256)S(1)} %pad_maximum_fusion.6, f32[3,8,9,1,256]{4,2,0,1,3:T(8,128)S(1)} %maximum_add_fusion.1, f32[3,8,1,9,256]{4,2,0,1,3:T(1,128)S(1)} %get-tuple-element.32, ...), kind=kOutput, calls=%fused_computation.48 | convolution fusion | flops 61212672 | bytes 8408932 | tf_op jit(solution)/shard_map/ji,pejbl->peibl/dot_general | solution.py:109
  316.5 14.7 %all-reduce.1 = (f32[3,256]{1,0:T(4,128)}, f32[3,256]{1,0:T(4,128)}) all-reduce(f32[3,256]{1,0:T(4,128)} %get-tuple-element.8, f32[3,256]{1,0:T(4,128)} %get-tuple-element.7), channel_id=1, replica_groups=mesh['elem'=8,'mode'=4] {'elem'}, use_global_device_ids=true, to_apply=%region_4.5 | all-reduce | flops 1536 | bytes 12288 | tf_op jit(solution)/shard_map/psum | solution.py:123
  332.5 5.0 %multiply_subtract_fusion = (f32[3,8,9,9,256]{4,2,3,1,0:T(8,128)S(1)}, f32[3,8,9,9,256]{4,2,3,1,0:T(8,128)}) fusion(f32[3,256]{1,0:T(4,128)S(1)} %get-tuple-element.14, f32[3,8,9,9,256]{4,2,0,1,3:T(8,128)S(1)} %fusion.25, f32[3,8,9,1,256]{4,2,3,1,0:T(8,128)} %copy-done.7, f32[3,7,9,256]{3,2,0,1:T(8,128)} %copy-done.12, f32[3,1,9,256]{3,2,0,1:T(8,128)} %copy-done.14, ...), kind=kLoop, calls=%fused_computation.72 | loop fusion | flops 2543616 | bytes 7965696 | tf_op jit(solution)/shard_map/sub | solution.py:208
  337.5 4.9 %fusion.39 = f32[3,8,9,256,9]{3,4,2,1,0:T(8,128)S(1)} fusion(f32[9,9,1,1,1]{1,0,4,3,2:T(8,128)S(1)} %copy-done.13, f32[3,8,9,9,256]{4,2,3,1,0:T(8,128)S(1)} %get-tuple-element.25), kind=kOutput, calls=%fused_computation.58 | convolution fusion | flops 53747712 | bytes 3981636 | tf_op jit(solution)/shard_map/ij,peajl->peail/dot_general | solution.py:106
  350.0 5.2 %fusion.27 = f32[3,8,9,9,256]{4,2,0,1,3:T(8,128)S(1)} fusion(f32[3,8,9,256,9]{3,4,2,1,0:T(8,128)S(1)} %fusion.28, f32[3,8,9,9,256]{4,2,3,1,0:T(8,128)S(1)} %get-tuple-element.25, f32[9,9,1,1,1]{1,0,2,3,4:T(8,128)S(1)} %copy-done.29, f32[3,8,9,9,256]{4,2,3,1,0:T(8,128)S(1)} %fusion.30, f32[256]{0:T(256)S(1)} %copy-done.40, f32[8,9,9]{1,0,2:T(8,128)S(1)} %copy-done.15), kind=kOutput, calls=%fused_computation.41 | convolution fusion | flops 56236032 | bytes 7966564 | tf_op jit(solution)/shard_map/ji,pejbl->peibl/dot_general | solution.py:109
  363.8 4.8 %concatenate.89 = f32[3,648,2,128]{3,2,0,1:T(2,128)} reshape(f32[3,8,9,9,256]{4,0,3,2,1:T(4,128)} %copy.136) | data formatting | bytes 3981312 | tf_op jit(solution)/shard_map/concatenate | solution.py:94
  370.3 5.0 %copy.155 = f32[3,8,9,9,256]{4,0,3,2,1:T(4,128)} copy(f32[3,8,9,9,256]{4,2,3,1,0:T(8,128)} %get-tuple-element.26) | data formatting | bytes 3981312 | tf_op jit(solution)/shard_map/concatenate | solution.py:94
  385.7 12.0 %all-reduce = (f32[3,256]{1,0:T(4,128)S(1)}, f32[3,256]{1,0:T(4,128)S(1)}) all-reduce(f32[3,256]{1,0:T(4,128)S(1)} %get-tuple-element.6, f32[3,256]{1,0:T(4,128)S(1)} %get-tuple-element.5), channel_id=1, replica_groups=mesh['elem'=8,'mode'=4] {'elem'}, use_global_device_ids=true, to_apply=%region_8.9 | all-reduce | flops 1536 | bytes 12288 | tf_op jit(solution)/shard_map/psum | solution.py:123
  (182 shorter events, 120.6 us)
Async XLA Ops:
  0.0 10.6 %copy-start.37 = (f32[9]{0:T(128)S(1)}, f32[9]{0:T(128)}, u32[]{:S(2)}) copy-start(f32[9]{0:T(128)} %constant.72.clone) | copy-start | bytes 112
  0.0 10.7 %copy-start.38 = (f32[8]{0:T(128)S(1)}, f32[8]{0:T(128)}, u32[]{:S(2)}) copy-start(f32[8]{0:T(128)} %param.8) | copy-start | bytes 100
  0.0 10.7 %copy-start.35 = (s32[8]{0:T(128)S(1)}, s32[8]{0:T(128)}, u32[]{:S(2)}) copy-start(s32[8]{0:T(128)} %param.9) | copy-start | bytes 100
  3.6 52.3 %all-to-all-start = ((f32[3,648,2,128]{3,2,0,1:T(2,128)}), f32[3,648,2,128]{3,2,0,1:T(2,128)S(1)}, u32[]{:S(2)}, u32[]{:S(2)}) async-start(f32[3,648,2,128]{3,2,0,1:T(2,128)} %copy.119), calls=%async_computation | async-start | bytes 3981312 | tf_op jit(solution)/shard_map/all_to_all | solution.py:152
  10.7 31.0 %copy-start.16 = (f32[9,9]{1,0:T(8,128)}, f32[9,9]{1,0:T(8,128)S(1)}, u32[]{:S(2)}) copy-start(f32[9,9]{1,0:T(8,128)S(1)} %copy.118) | copy-start | bytes 976
  13.6 65.5 %copy-start.21 = (f32[1536]{0:T(1024)}, f32[1536]{0:T(1024)S(1)}, u32[]{:S(2)}) copy-start(f32[1536]{0:T(1024)S(1)} %fusion.76) | copy-start | bytes 18436
  106.3 19.2 %copy-start.13 = (f32[9,9,1,1,1]{1,0,4,3,2:T(8,128)S(1)}, f32[9,9,1,1,1]{1,0,4,3,2:T(8,128)}, u32[]{:S(2)}) copy-start(f32[9,9,1,1,1]{1,0,4,3,2:T(8,128)} %constant.74) | copy-start | bytes 976
  125.6 11.5 %copy-start.2 = (f32[3,162,1536]{2,0,1:T(4,128)S(1)}, f32[3,162,1536]{2,0,1:T(4,128)}, u32[]{:S(2)}) copy-start(f32[3,162,1536]{2,0,1:T(4,128)} %copy.122) | copy-start | bytes 8957956
  125.6 11.5 %copy-start.3 = (f32[2,9,9,1536]{3,1,2,0:T(8,128)S(1)}, f32[2,9,9,1536]{3,1,2,0:T(8,128)}, u32[]{:S(2)}) copy-start(f32[2,9,9,1536]{3,1,2,0:T(8,128)} %copy.127) | copy-start | bytes 2985988
  125.6 11.5 %copy-start.5 = (f32[3,162,1536]{2,0,1:T(4,128)S(1)}, f32[3,162,1536]{2,0,1:T(4,128)}, u32[]{:S(2)}) copy-start(f32[3,162,1536]{2,0,1:T(4,128)} %copy.128) | copy-start | bytes 8957956
  125.6 11.5 %copy-start.30 = (f32[2]{0:T(128)S(1)}, f32[2]{0:T(128)}, u32[]{:S(2)}) copy-start(f32[2]{0:T(128)} %get-tuple-element.62) | copy-start | bytes 28
  182.5 73.1 %all-to-all-start.1 = ((f32[3,162,2,512]{1,2,0,3:T(2,128)}), f32[3,162,2,512]{1,2,0,3:T(2,128)}, u32[]{:S(2)}, u32[]{:S(2)}) async-start(f32[3,162,2,512]{1,2,0,3:T(2,128)} %copy.132), calls=%async_computation.1 | async-start | bytes 6291456 | tf_op jit(solution)/shard_map/all_to_all | solution.py:184
  275.5 6.8 %collective-permute-start = (f32[3,8,1,9,256]{4,2,0,1,3:T(1,128)S(1)}, f32[3,8,1,9,256]{4,2,0,1,3:T(1,128)S(1)}, u32[]{:S(2)}, u32[]{:S(2)}) collective-permute-start(f32[3,8,1,9,256]{4,2,0,1,3:T(1,128)S(1)} %get-tuple-element.33), channel_id=1, source_target_pairs={{0,4},{4,8},{8,12},{12,16},{16,20},{20,24},{24,28},{28,0},{1,5},{5... | collective-permute-start | bytes 663560 | tf_op jit(solution)/shard_map/ppermute | solution.py:45
  275.6 6.8 %collective-permute-start.1 = (f32[3,8,1,9,256]{4,2,0,1,3:T(1,128)S(1)}, f32[3,8,1,9,256]{4,2,0,1,3:T(1,128)S(1)}, u32[]{:S(2)}, u32[]{:S(2)}) collective-permute-start(f32[3,8,1,9,256]{4,2,0,1,3:T(1,128)S(1)} %get-tuple-element.34), channel_id=1, source_target_pairs={{4,0},{8,4},{12,8},{16,12},{20,16},{24,20},{28,24},{0,28},{5,1},{9... | collective-permute-start | bytes 663560 | tf_op jit(solution)/shard_map/ppermute | solution.py:46
  278.2 19.9 %copy-start.39 = (f32[256]{0:T(256)}, f32[256]{0:T(256)S(1)}, u32[]{:S(2)}) copy-start(f32[256]{0:T(256)S(1)} %pad_maximum_fusion.6) | copy-start | bytes 3076
  298.1 9.1 %copy-start.36 = (f32[9]{0:T(128)S(1)}, f32[9]{0:T(128)}, u32[]{:S(2)}) copy-start(f32[9]{0:T(128)} %or_select_fusion) | copy-start | bytes 112
  304.3 7.6 %collective-permute-start.2 = (f32[3,8,1,9,256]{4,2,0,1,3:T(1,128)S(1)}, f32[3,8,1,9,256]{4,2,0,1,3:T(1,128)S(1)}, u32[]{:S(2)}, u32[]{:S(2)}) collective-permute-start(f32[3,8,1,9,256]{4,2,0,1,3:T(1,128)S(1)} %get-tuple-element.29), channel_id=1, source_target_pairs={{0,4},{4,8},{8,12},{12,16},{16,20},{20,24},{24,28},{28,0},{1,5},{5... | collective-permute-start | bytes 663560 | tf_op jit(solution)/shard_map/ppermute | solution.py:45
  306.1 5.8 %collective-permute-start.3 = (f32[3,8,1,9,256]{4,2,0,1,3:T(1,128)S(1)}, f32[3,8,1,9,256]{4,2,0,1,3:T(1,128)S(1)}, u32[]{:S(2)}, u32[]{:S(2)}) collective-permute-start(f32[3,8,1,9,256]{4,2,0,1,3:T(1,128)S(1)} %get-tuple-element.30), channel_id=1, source_target_pairs={{4,0},{8,4},{12,8},{16,12},{20,16},{24,20},{28,24},{0,28},{5,1},{9... | collective-permute-start | bytes 663560 | tf_op jit(solution)/shard_map/ppermute | solution.py:46
  337.5 12.5 %copy-start = (f32[3,8,9,9,256]{4,2,3,1,0:T(8,128)}, f32[3,8,9,9,256]{4,2,3,1,0:T(8,128)S(1)}, u32[]{:S(2)}) copy-start(f32[3,8,9,9,256]{4,2,3,1,0:T(8,128)S(1)} %get-tuple-element.25) | copy-start | bytes 5971972
  358.2 21.6 %collective-permute-start.4 = (f32[3,8,1,9,256]{4,2,0,1,3:T(1,128)}, f32[3,8,1,9,256]{4,2,0,1,3:T(1,128)}, u32[]{:S(2)}, u32[]{:S(2)}) collective-permute-start(f32[3,8,1,9,256]{4,2,0,1,3:T(1,128)} %get-tuple-element.23), channel_id=1, source_target_pairs={{0,4},{4,8},{8,12},{12,16},{16,20},{20,24},{24,28},{28,0},{1,5},{5... | collective-permute-start | bytes 663560 | tf_op jit(solution)/shard_map/ppermute | solution.py:45
  358.2 21.6 %collective-permute-start.5 = (f32[3,8,1,9,256]{4,2,0,1,3:T(1,128)}, f32[3,8,1,9,256]{4,2,0,1,3:T(1,128)}, u32[]{:S(2)}, u32[]{:S(2)}) collective-permute-start(f32[3,8,1,9,256]{4,2,0,1,3:T(1,128)} %get-tuple-element.24), channel_id=1, source_target_pairs={{4,0},{8,4},{12,8},{16,12},{20,16},{24,20},{28,24},{0,28},{5,1},{9... | collective-permute-start | bytes 663560 | tf_op jit(solution)/shard_map/ppermute | solution.py:46
  363.8 6.5 %copy-start.24 = (f32[3,256]{1,0:T(4,128)S(1)}, f32[3,256]{1,0:T(4,128)}, u32[]{:S(2)}) copy-start(f32[3,256]{1,0:T(4,128)} %copy-done.23) | copy-start | bytes 9220
  384.3 13.4 %copy-start.26 = (f32[3,256]{1,0:T(4,128)S(1)}, f32[3,256]{1,0:T(4,128)}, u32[]{:S(2)}) copy-start(f32[3,256]{1,0:T(4,128)} %get-tuple-element.11) | copy-start | bytes 9220
  384.3 13.4 %copy-start.27 = (f32[3,256]{1,0:T(4,128)S(1)}, f32[3,256]{1,0:T(4,128)}, u32[]{:S(2)}) copy-start(f32[3,256]{1,0:T(4,128)} %get-tuple-element.12) | copy-start | bytes 9220
  (25 other events, 88.8 us)
where the time goes:
time: 409 us; the launch traced here: 404 us
  matrix products  106 us (26%)
  local copies, waits for them, and re-layouts  84.7 us (21%)
  other arithmetic  79.2 us (19%)
  waiting for transfers between devices  71.7 us (18%)
  blocking collectives  39.5 us (10%)
  starting transfers between devices  19.2 us (5%)
    all_to_all x1, waiting for transfers between devices, on_device(): lax.all_to_all(spectral, 'mode', split_axis=3, concat_axis=1, tiled=True)  63.4 us
    psum x2, blocking collectives, paired(): lax.psum((weighted_sum(residual, residual, multiplicity), weighted_sum(re...  26.7 us
    concatenate x4, local copies, waits for them, and re-layouts, assemble(): jnp.concatenate([jnp.roll(upper_layer, 1, axis=1)[:, :, :, None], nodal_f...  17.2 us
    dot_general x1, matrix products, on_device(): jnp.einsum('peabq,ql->peabl', tendency, forward, precision=highest)  17.1 us
    dot_general x1, matrix products, on_device(): jnp.einsum('ij,pejbq->peibq', derivative, values, precision=highest)  14.2 us
    mul x2, other arithmetic, spectral_tables(): -wave_number * mode_weight * sine_table  14.2 us
    mul x1, other arithmetic, spectral_tables(): -mode_weight * sine_table  14.2 us
    cos x1, other arithmetic, spectral_tables(): cosine_table = jnp.cos(angles)  14 us
  transfers between devices with their start and end apart: 8, of which 3 were waited for; matrix products, arithmetic and copies ran while one was open for 17% of the time, Pallas kernels for 0%

commit v1 on v0

--- a/solution.py
+++ b/solution.py
@@ -181,7 +181,9 @@
     tendency = jnp.concatenate([(thrust - advection[0])[None], -advection[1:]], axis=0)
     spectral = jnp.einsum("peabq,ql->peabl", tendency, forward, precision=highest)
     spectral = spectral.reshape(3, local_elems * 81, 2, mode_count)
-    returned = lax.all_to_all(spectral, "mode", split_axis=3, concat_axis=1, tiled=True)
+    pieces = jnp.split(spectral, lax.axis_size("mode"), axis=3)
+    received = lax.all_to_all(jnp.stack(pieces), "mode", 0, 0)
+    returned = jnp.concatenate(received, axis=1)
     u_star = nodal_field + time_step * returned.reshape(3, elements, 9, 9, 2 * local_modes)
     jacobian = col_width * row_height / 4.0
     ratio_x = row_height / col_width

time: 409 us -> 374 us (0.914)
  waiting for transfers between devices: 71.7 us -> 47 us
  local copies, waits for them, and re-layouts: 84.7 us -> 73.9 us
    all_to_all x1, waiting for transfers between devices: 63.4 us -> 38.6 us  [on_device(): received = lax.all_to_all(jnp.stack(pieces), 'mode', 0, 0)]
    reshape x2 -> x1, local copies, waits for them, and re-layouts: 9.69 us -> 3.12 us  [on_device(): spectral = spectral.reshape(3, local_elems * 81, 2, mode_count)]
    mul x2 -> x1, local copies, waits for them, and re-layouts: 11.1 us -> 4.67 us  [on_device(): time_step * returned.reshape(3, elements, 9, 9, 2 * local_modes)]
  transfers between devices with their start and end apart: 8 -> 8, of which waited for: 3 -> 4; matrix products, arithmetic and copies ran while one was open for 17% -> 19% of each run, Pallas kernels for 0% -> 0%
where the time goes in v1:
time: 374 us; the launch traced here: 369 us
  matrix products  106 us (28%)
  other arithmetic  79.8 us (21%)
  local copies, waits for them, and re-layouts  73.9 us (20%)
  waiting for transfers between devices  47 us (13%)
  blocking collectives  39.5 us (11%)
  starting transfers between devices  19 us (5%)
    all_to_all x1, waiting for transfers between devices, on_device(): received = lax.all_to_all(jnp.stack(pieces), 'mode', 0, 0)  38.6 us
    psum x2, blocking collectives, paired(): lax.psum((weighted_sum(residual, residual, multiplicity), weighted_sum(re...  26.7 us
    concatenate x4, local copies, waits for them, and re-layouts, assemble(): jnp.concatenate([jnp.roll(upper_layer, 1, axis=1)[:, :, :, None], nodal_f...  17.2 us
    dot_general x1, matrix products, on_device(): jnp.einsum('peabq,ql->peabl', tendency, forward, precision=highest)  17.1 us
    dot_general x1, matrix products, on_device(): jnp.einsum('ij,pejbq->peibq', derivative, values, precision=highest)  14.2 us
    mul x1, other arithmetic, spectral_tables(): -mode_weight * sine_table  14.2 us
    mul x2, other arithmetic, spectral_tables(): -wave_number * mode_weight * sine_table  14.2 us
    cos x1, other arithmetic, spectral_tables(): cosine_table = jnp.cos(angles)  14 us
  transfers between devices with their start and end apart: 8, of which 4 were waited for; matrix products, arithmetic and copies ran while one was open for 19% of the time, Pallas kernels for 0%

profile of v1, /device:TPU:0, one launch (start us, length us, event | category | flops | bytes accessed | tf_op | source)
XLA Modules:
  0.0 368.7 jit_solution(5086426370864941260)
XLA Ops:
  3.6 6.3 %all-to-all-start = ((f32[3,648,2,128]{3,2,0,1:T(2,128)}), f32[3,648,2,128]{3,2,0,1:T(2,128)S(1)}, u32[]{:S(2)}, u32[]{:S(2)}) async-start(f32[3,648,2,128]{3,2,0,1:T(2,128)} %copy.78), calls=%async_computation | async-start | bytes 3981312 | tf_op jit(solution)/shard_map/all_to_all | solution.py:152
  13.4 14.0 %fusion.61 = (f32[512,1536]{1,0:T(8,128)}, f32[512,1536]{1,0:T(8,128)}) fusion(), kind=kLoop, calls=%fused_computation.87 | loop fusion | flops 7864320 | bytes 6291456 | tf_op jit(solution)/shard_map/cos | solution.py:70
  27.4 14.2 %fusion.63 = (f32[512,1536]{1,0:T(8,128)}, f32[512,1536]{1,0:T(8,128)}) fusion(f32[512]{0:T(512)S(1)} %negate_multiply_fusion), kind=kLoop, calls=%fused_computation.89 | loop fusion | flops 8650752 | bytes 6293504 | tf_op jit(solution)/shard_map/mul | solution.py:78
  41.6 14.2 %fusion.64 = (f32[512,1536]{1,0:T(8,128)}, f32[512,1536]{1,0:T(8,128)}) fusion(f32[512]{0:T(512)S(1)} %fusion.77, f32[512]{0:T(512)S(1)} %select_multiply_fusion), kind=kLoop, calls=%fused_computation.90 | loop fusion | flops 8650752 | bytes 6295552 | tf_op jit(solution)/shard_map/mul | solution.py:76
  61.2 13.4 %fusion.54 = f32[3,162,1536]{2,1,0:T(8,128)S(1)} fusion(f32[3,162,1024]{2,1,0:T(8,128)} %reshape.202, f32[512,1536]{1,0:T(8,128)S(1)} %copy-done.11, f32[512,1536]{1,0:T(8,128)} %get-tuple-element.68), kind=kOutput, calls=%fused_computation.79 | convolution fusion | flops 9174515712 | bytes 11268096 | tf_op jit(solution)/shard_map/pnl,lq->pnq/dot_general | solution.py:154
  92.9 13.4 %fusion.53 = f32[3,162,1536]{2,1,0:T(8,128)S(1)} fusion(f32[3,162,1024]{2,1,0:T(8,128)} %reshape.202, f32[512,1536]{1,0:T(8,128)} %get-tuple-element.60, f32[512,1536]{1,0:T(8,128)S(1)} %copy-done.10), kind=kOutput, calls=%fused_computation.78 | convolution fusion | flops 9174515712 | bytes 11268096 | tf_op jit(solution)/shard_map/pnl,lq->pnq/dot_general | solution.py:155
  110.6 12.7 %psum.35 = f32[]{:T(128)} all-reduce(f32[]{:T(128)} %get-tuple-element.35), channel_id=1, replica_groups=mesh['elem'=8,'mode'=4] {'mode'}, use_global_device_ids=true, to_apply=%region_1.2 | all-reduce | flops 1 | bytes 8 | tf_op jit(solution)/shard_map/psum | solution.py:171
  125.5 11.5 %fusion.16 = f32[3,2,9,1536,9]{3,4,2,1,0:T(8,128)} fusion(f32[9,9,1,1,1]{1,0,4,3,2:T(8,128)S(1)} %copy-done.13, f32[3,2,9,9,1536]{4,0,3,2,1:T(4,128)} %bitcast.145), kind=kOutput, calls=%fused_computation.24 | convolution fusion | flops 80621568 | bytes 5972292 | tf_op jit(solution)/shard_map/ij,peajq->peaiq/dot_general | solution.py:159
  137.0 14.2 %fusion.15 = f32[3,2,9,9,1536]{4,2,3,1,0:T(8,128)S(1)} fusion(f32[3,2,9,9,1536]{4,0,3,2,1:T(4,128)S(1)} %bitcast.147, f32[3,2,9,1536,9]{3,4,2,1,0:T(8,128)} %fusion.16, f32[9,9,1,1,1]{1,0,4,3,2:T(8,128)S(1)} %copy-done.13, f32[3,2,9,9,1536]{4,0,3,2,1:T(4,128)S(1)} %bitcast.146, f32[2,9,9,1536]{3,1,2,0:T(8,128)S(1)} %copy-done.3, f32[2]{0:T(128)S(1)} %copy-done.30, ...), kind=kOutput, calls=%fused_computation.20 | convolution fusion | flops 85847040 | bytes 14930256 | tf_op jit(solution)/shard_map/ij,pejbq->peibq/dot_general | solution.py:158
  154.2 17.1 %fusion.7 = f32[3,2,9,9,1024]{4,2,3,1,0:T(8,128)S(1)} fusion(f32[512,1536]{1,0:T(8,128)S(1)} %copy-done.9, f32[512,1536]{1,0:T(8,128)S(1)} %copy-done.8, f32[2,2,9,9,1536]{4,2,3,1,0:T(8,128)S(1)} %slice_negate_fusion, f32[1,2,9,9,1536]{4,2,3,1,0:T(8,128)S(1)} %slice_subtract_fusion), kind=kOutput, calls=%fused_computation.10 | convolution fusion | flops 9176835072 | bytes 11268096 | tf_op jit(solution)/shard_map/peabq,ql->peabl/dot_general | solution.py:182
  180.1 4.4 %all-to-all-start.1 = ((f32[4,3,162,2,128]{4,3,1,2,0:T(2,128)}), f32[4,3,162,2,128]{4,3,1,2,0:T(2,128)}, u32[]{:S(2)}, u32[]{:S(2)}) async-start(f32[4,3,162,2,128]{4,3,1,2,0:T(2,128)} %pad_maximum_fusion.3), calls=%async_computation.1 | async-start | bytes 3981312 | tf_op jit(solution)/shard_map/all_to_all | solution.py:185
  189.6 38.6 %all-to-all-done.1 = f32[4,3,162,2,128]{4,3,1,2,0:T(2,128)} async-done(((f32[4,3,162,2,128]{4,3,1,2,0:T(2,128)}), f32[4,3,162,2,128]{4,3,1,2,0:T(2,128)}, u32[]{:S(2)}, u32[]{:S(2)}) %all-to-all-start.1) | async-done | bytes 1990688 | tf_op jit(solution)/shard_map/all_to_all | solution.py:185
  232.0 4.7 %mul.651 = f32[3,8,9,9,256]{4,0,3,2,1:T(4,128)} reshape(f32[3,4,162,2,128]{4,3,0,2,1:T(2,128)} %multiply_bitcast_fusion) | data formatting | bytes 3981312 | tf_op jit(solution)/shard_map/mul | solution.py:187
  249.8 4.9 %fusion.46 = f32[3,8,9,256,9]{3,4,2,1,0:T(8,128)S(1)} fusion(f32[9,9,1,1,1]{1,0,4,3,2:T(8,128)S(1)} %copy-done.13, f32[3,8,9,9,256]{4,2,3,1,0:T(8,128)S(1)} %copy_multiply_fusion.4), kind=kOutput, calls=%fused_computation.66 | convolution fusion | flops 53747712 | bytes 3981636 | tf_op jit(solution)/shard_map/ij,peajl->peail/dot_general | solution.py:106
  262.9 5.9 %fusion.32 = f32[3,8,9,9,256]{4,2,0,1,3:T(8,128)S(1)} fusion(f32[3,8,9,256,9]{3,4,2,1,0:T(8,128)S(1)} %fusion.33, f32[8,9,9]{1,0,2:T(8,128)S(1)} %copy-done.22, f32[256]{0:T(256)S(1)} %pad_maximum_fusion.7, f32[3,8,9,1,256]{4,2,0,1,3:T(8,128)S(1)} %maximum_add_fusion.1, f32[3,8,1,9,256]{4,2,0,1,3:T(1,128)S(1)} %get-tuple-element.32, ...), kind=kOutput, calls=%fused_computation.48 | convolution fusion | flops 61212672 | bytes 8408932 | tf_op jit(solution)/shard_map/ji,pejbl->peibl/dot_general | solution.py:109
  272.3 4.4 %collective-permute-done.2 = f32[3,8,1,9,256]{4,2,0,1,3:T(1,128)S(1)} collective-permute-done((f32[3,8,1,9,256]{4,2,0,1,3:T(1,128)S(1)}, f32[3,8,1,9,256]{4,2,0,1,3:T(1,128)S(1)}, u32[]{:S(2)}, u32[]{:S(2)}) %collective-permute-start.2) | collective-permute-done | bytes 221216 | tf_op jit(solution)/shard_map/ppermute | solution.py:45
  281.3 14.7 %all-reduce.1 = (f32[3,256]{1,0:T(4,128)}, f32[3,256]{1,0:T(4,128)}) all-reduce(f32[3,256]{1,0:T(4,128)} %get-tuple-element.8, f32[3,256]{1,0:T(4,128)} %get-tuple-element.7), channel_id=1, replica_groups=mesh['elem'=8,'mode'=4] {'elem'}, use_global_device_ids=true, to_apply=%region_4.5 | all-reduce | flops 1536 | bytes 12288 | tf_op jit(solution)/shard_map/psum | solution.py:123
  297.3 5.0 %multiply_subtract_fusion = (f32[3,8,9,9,256]{4,2,3,1,0:T(8,128)S(1)}, f32[3,8,9,9,256]{4,2,3,1,0:T(8,128)}) fusion(f32[3,256]{1,0:T(4,128)S(1)} %get-tuple-element.14, f32[3,8,9,9,256]{4,2,0,1,3:T(8,128)S(1)} %fusion.25, f32[3,8,9,1,256]{4,2,3,1,0:T(8,128)} %copy-done.7, f32[3,7,9,256]{3,2,0,1:T(8,128)} %copy-done.12, f32[3,1,9,256]{3,2,0,1:T(8,128)} %copy-done.14, ...), kind=kLoop, calls=%fused_computation.72 | loop fusion | flops 2543616 | bytes 7965696 | tf_op jit(solution)/shard_map/sub | solution.py:210
  302.3 4.9 %fusion.43 = f32[3,8,9,256,9]{3,4,2,1,0:T(8,128)S(1)} fusion(f32[9,9,1,1,1]{1,0,4,3,2:T(8,128)S(1)} %copy-done.13, f32[3,8,9,9,256]{4,2,3,1,0:T(8,128)S(1)} %get-tuple-element.25), kind=kOutput, calls=%fused_computation.62 | convolution fusion | flops 53747712 | bytes 3981636 | tf_op jit(solution)/shard_map/ij,peajl->peail/dot_general | solution.py:106
  314.8 5.2 %fusion.27 = f32[3,8,9,9,256]{4,2,0,1,3:T(8,128)S(1)} fusion(f32[3,8,9,256,9]{3,4,2,1,0:T(8,128)S(1)} %fusion.28, f32[3,8,9,9,256]{4,2,3,1,0:T(8,128)S(1)} %get-tuple-element.25, f32[9,9,1,1,1]{1,0,2,3,4:T(8,128)S(1)} %copy-done.29, f32[3,8,9,9,256]{4,2,3,1,0:T(8,128)S(1)} %fusion.30, f32[256]{0:T(256)S(1)} %copy-done.40, f32[8,9,9]{1,0,2:T(8,128)S(1)} %copy-done.15), kind=kOutput, calls=%fused_computation.41 | convolution fusion | flops 56236032 | bytes 7966564 | tf_op jit(solution)/shard_map/ji,pejbl->peibl/dot_general | solution.py:109
  328.6 4.8 %concatenate.89 = f32[3,648,2,128]{3,2,0,1:T(2,128)} reshape(f32[3,8,9,9,256]{4,0,3,2,1:T(4,128)} %copy.93) | data formatting | bytes 3981312 | tf_op jit(solution)/shard_map/concatenate | solution.py:94
  335.1 5.0 %copy.112 = f32[3,8,9,9,256]{4,0,3,2,1:T(4,128)} copy(f32[3,8,9,9,256]{4,2,3,1,0:T(8,128)} %get-tuple-element.26) | data formatting | bytes 3981312 | tf_op jit(solution)/shard_map/concatenate | solution.py:94
  340.1 4.5 %concatenate.105 = f32[3,648,2,128]{3,2,0,1:T(2,128)} reshape(f32[3,8,9,9,256]{4,0,3,2,1:T(4,128)} %copy.112) | data formatting | bytes 3981312 | tf_op jit(solution)/shard_map/concatenate | solution.py:94
  350.5 12.0 %all-reduce = (f32[3,256]{1,0:T(4,128)S(1)}, f32[3,256]{1,0:T(4,128)S(1)}) all-reduce(f32[3,256]{1,0:T(4,128)S(1)} %get-tuple-element.6, f32[3,256]{1,0:T(4,128)S(1)} %get-tuple-element.5), channel_id=1, replica_groups=mesh['elem'=8,'mode'=4] {'elem'}, use_global_device_ids=true, to_apply=%region_8.9 | all-reduce | flops 1536 | bytes 12288 | tf_op jit(solution)/shard_map/psum | solution.py:123
  (182 shorter events, 115.2 us)
Async XLA Ops:
  0.0 10.6 %copy-start.37 = (f32[9]{0:T(128)S(1)}, f32[9]{0:T(128)}, u32[]{:S(2)}) copy-start(f32[9]{0:T(128)} %constant.72.clone) | copy-start | bytes 112
  0.0 10.7 %copy-start.38 = (f32[8]{0:T(128)S(1)}, f32[8]{0:T(128)}, u32[]{:S(2)}) copy-start(f32[8]{0:T(128)} %param.8) | copy-start | bytes 100
  0.0 10.7 %copy-start.35 = (s32[8]{0:T(128)S(1)}, s32[8]{0:T(128)}, u32[]{:S(2)}) copy-start(s32[8]{0:T(128)} %param.9) | copy-start | bytes 100
  3.6 52.3 %all-to-all-start = ((f32[3,648,2,128]{3,2,0,1:T(2,128)}), f32[3,648,2,128]{3,2,0,1:T(2,128)S(1)}, u32[]{:S(2)}, u32[]{:S(2)}) async-start(f32[3,648,2,128]{3,2,0,1:T(2,128)} %copy.78), calls=%async_computation | async-start | bytes 3981312 | tf_op jit(solution)/shard_map/all_to_all | solution.py:152
  10.7 30.8 %copy-start.16 = (f32[9,9]{1,0:T(8,128)}, f32[9,9]{1,0:T(8,128)S(1)}, u32[]{:S(2)}) copy-start(f32[9,9]{1,0:T(8,128)S(1)} %copy.77) | copy-start | bytes 976
  13.4 65.6 %copy-start.21 = (f32[1536]{0:T(1024)}, f32[1536]{0:T(1024)S(1)}, u32[]{:S(2)}) copy-start(f32[1536]{0:T(1024)S(1)} %fusion.76) | copy-start | bytes 18436
  106.3 19.2 %copy-start.13 = (f32[9,9,1,1,1]{1,0,4,3,2:T(8,128)S(1)}, f32[9,9,1,1,1]{1,0,4,3,2:T(8,128)}, u32[]{:S(2)}) copy-start(f32[9,9,1,1,1]{1,0,4,3,2:T(8,128)} %constant.74) | copy-start | bytes 976
  125.5 11.5 %copy-start.2 = (f32[3,162,1536]{2,0,1:T(4,128)S(1)}, f32[3,162,1536]{2,0,1:T(4,128)}, u32[]{:S(2)}) copy-start(f32[3,162,1536]{2,0,1:T(4,128)} %copy.81) | copy-start | bytes 8957956
  125.5 11.5 %copy-start.3 = (f32[2,9,9,1536]{3,1,2,0:T(8,128)S(1)}, f32[2,9,9,1536]{3,1,2,0:T(8,128)}, u32[]{:S(2)}) copy-start(f32[2,9,9,1536]{3,1,2,0:T(8,128)} %copy.86) | copy-start | bytes 2985988
  125.5 11.5 %copy-start.5 = (f32[3,162,1536]{2,0,1:T(4,128)S(1)}, f32[3,162,1536]{2,0,1:T(4,128)}, u32[]{:S(2)}) copy-start(f32[3,162,1536]{2,0,1:T(4,128)} %copy.87) | copy-start | bytes 8957956
  125.5 11.5 %copy-start.30 = (f32[2]{0:T(128)S(1)}, f32[2]{0:T(128)}, u32[]{:S(2)}) copy-start(f32[2]{0:T(128)} %get-tuple-element.66) | copy-start | bytes 28
  180.1 48.1 %all-to-all-start.1 = ((f32[4,3,162,2,128]{4,3,1,2,0:T(2,128)}), f32[4,3,162,2,128]{4,3,1,2,0:T(2,128)}, u32[]{:S(2)}, u32[]{:S(2)}) async-start(f32[4,3,162,2,128]{4,3,1,2,0:T(2,128)} %pad_maximum_fusion.3), calls=%async_computation.1 | async-start | bytes 3981312 | tf_op jit(solution)/shard_map/all_to_all | solution.py:185
  240.3 6.8 %collective-permute-start = (f32[3,8,1,9,256]{4,2,0,1,3:T(1,128)S(1)}, f32[3,8,1,9,256]{4,2,0,1,3:T(1,128)S(1)}, u32[]{:S(2)}, u32[]{:S(2)}) collective-permute-start(f32[3,8,1,9,256]{4,2,0,1,3:T(1,128)S(1)} %get-tuple-element.33), channel_id=1, source_target_pairs={{0,4},{4,8},{8,12},{12,16},{16,20},{20,24},{24,28},{28,0},{1,5},{5... | collective-permute-start | bytes 663560 | tf_op jit(solution)/shard_map/ppermute | solution.py:45
  240.3 6.8 %collective-permute-start.1 = (f32[3,8,1,9,256]{4,2,0,1,3:T(1,128)S(1)}, f32[3,8,1,9,256]{4,2,0,1,3:T(1,128)S(1)}, u32[]{:S(2)}, u32[]{:S(2)}) collective-permute-start(f32[3,8,1,9,256]{4,2,0,1,3:T(1,128)S(1)} %get-tuple-element.34), channel_id=1, source_target_pairs={{4,0},{8,4},{12,8},{16,12},{20,16},{24,20},{28,24},{0,28},{5,1},{9... | collective-permute-start | bytes 663560 | tf_op jit(solution)/shard_map/ppermute | solution.py:46
  243.0 19.9 %copy-start.39 = (f32[256]{0:T(256)}, f32[256]{0:T(256)S(1)}, u32[]{:S(2)}) copy-start(f32[256]{0:T(256)S(1)} %pad_maximum_fusion.7) | copy-start | bytes 3076
  262.9 9.1 %copy-start.36 = (f32[9]{0:T(128)S(1)}, f32[9]{0:T(128)}, u32[]{:S(2)}) copy-start(f32[9]{0:T(128)} %or_select_fusion) | copy-start | bytes 112
  269.1 7.6 %collective-permute-start.2 = (f32[3,8,1,9,256]{4,2,0,1,3:T(1,128)S(1)}, f32[3,8,1,9,256]{4,2,0,1,3:T(1,128)S(1)}, u32[]{:S(2)}, u32[]{:S(2)}) collective-permute-start(f32[3,8,1,9,256]{4,2,0,1,3:T(1,128)S(1)} %get-tuple-element.29), channel_id=1, source_target_pairs={{0,4},{4,8},{8,12},{12,16},{16,20},{20,24},{24,28},{28,0},{1,5},{5... | collective-permute-start | bytes 663560 | tf_op jit(solution)/shard_map/ppermute | solution.py:45
  270.9 5.8 %collective-permute-start.3 = (f32[3,8,1,9,256]{4,2,0,1,3:T(1,128)S(1)}, f32[3,8,1,9,256]{4,2,0,1,3:T(1,128)S(1)}, u32[]{:S(2)}, u32[]{:S(2)}) collective-permute-start(f32[3,8,1,9,256]{4,2,0,1,3:T(1,128)S(1)} %get-tuple-element.30), channel_id=1, source_target_pairs={{4,0},{8,4},{12,8},{16,12},{20,16},{24,20},{28,24},{0,28},{5,1},{9... | collective-permute-start | bytes 663560 | tf_op jit(solution)/shard_map/ppermute | solution.py:46
  302.3 12.5 %copy-start = (f32[3,8,9,9,256]{4,2,3,1,0:T(8,128)}, f32[3,8,9,9,256]{4,2,3,1,0:T(8,128)S(1)}, u32[]{:S(2)}) copy-start(f32[3,8,9,9,256]{4,2,3,1,0:T(8,128)S(1)} %get-tuple-element.25) | copy-start | bytes 5971972
  323.0 21.6 %collective-permute-start.4 = (f32[3,8,1,9,256]{4,2,0,1,3:T(1,128)}, f32[3,8,1,9,256]{4,2,0,1,3:T(1,128)}, u32[]{:S(2)}, u32[]{:S(2)}) collective-permute-start(f32[3,8,1,9,256]{4,2,0,1,3:T(1,128)} %get-tuple-element.23), channel_id=1, source_target_pairs={{0,4},{4,8},{8,12},{12,16},{16,20},{20,24},{24,28},{28,0},{1,5},{5... | collective-permute-start | bytes 663560 | tf_op jit(solution)/shard_map/ppermute | solution.py:45
  323.0 21.6 %collective-permute-start.5 = (f32[3,8,1,9,256]{4,2,0,1,3:T(1,128)}, f32[3,8,1,9,256]{4,2,0,1,3:T(1,128)}, u32[]{:S(2)}, u32[]{:S(2)}) collective-permute-start(f32[3,8,1,9,256]{4,2,0,1,3:T(1,128)} %get-tuple-element.24), channel_id=1, source_target_pairs={{4,0},{8,4},{12,8},{16,12},{20,16},{24,20},{28,24},{0,28},{5,1},{9... | collective-permute-start | bytes 663560 | tf_op jit(solution)/shard_map/ppermute | solution.py:46
  328.6 6.5 %copy-start.24 = (f32[3,256]{1,0:T(4,128)S(1)}, f32[3,256]{1,0:T(4,128)}, u32[]{:S(2)}) copy-start(f32[3,256]{1,0:T(4,128)} %copy-done.23) | copy-start | bytes 9220
  349.1 13.4 %copy-start.26 = (f32[3,256]{1,0:T(4,128)S(1)}, f32[3,256]{1,0:T(4,128)}, u32[]{:S(2)}) copy-start(f32[3,256]{1,0:T(4,128)} %get-tuple-element.11) | copy-start | bytes 9220
  349.2 13.4 %copy-start.27 = (f32[3,256]{1,0:T(4,128)S(1)}, f32[3,256]{1,0:T(4,128)}, u32[]{:S(2)}) copy-start(f32[3,256]{1,0:T(4,128)} %get-tuple-element.12) | copy-start | bytes 9220
  (25 other events, 88.8 us)
